TPU v7x, 32 devices: a whole 2x2x4 slice. The times are simulated.
32 devices in a mesh: wide: 8 (over z, x), narrow: 4 (over y, core).
Axes of the slice: x: 2, y: 2, z: 4, core: 2. Of those that a mesh axis runs over, the one named last changes fastest.
Arguments:
- tokens: bfloat16 [4096, 2048], P('wide', 'narrow'), may hold values from -6 to 6
- cotangent: bfloat16 [4096, 2048], P('wide', 'narrow'), may hold values from -6 to 6
- block_ids: int32 [8, 512], P('wide'), may hold values from 0 to 2, never falling along the last dimension, each value on 1 to 256 neighbouring positions
- routes: int32 [4096, 8], P('wide'), may hold values from 0 to 15, all different within a row; in each aligned block of 512 rows (0 to 511, 512 to 1023, ...) at most 272 rows name the same one
- norm_attn: bfloat16 [2048], P('narrow'), may hold values from 0.5 to 1.5
- w_query: bfloat16 [2048, 2048], P('wide', 'narrow'), may hold values from -0.125 to 0.125
- w_key: bfloat16 [2048, 2048], P('wide', 'narrow'), may hold values from -0.125 to 0.125
- w_value: bfloat16 [2048, 2048], P('wide', 'narrow'), may hold values from -0.125 to 0.125
- norm_query: bfloat16 [2048], P('narrow'), may hold values from 0.5 to 1.5
- norm_key: bfloat16 [2048], P('narrow'), may hold values from 0.5 to 1.5
- w_out: bfloat16 [2048, 2048], P('wide', 'narrow'), may hold values from -1 to 1
- norm_ffn: bfloat16 [2048], P('narrow'), may hold values from 0.5 to 1.5
- w_router: bfloat16 [2048, 16], replicated, may hold values from -0.0625 to 0.0625
- w_gate: bfloat16 [2048, 16, 1024], P('wide', None, 'narrow'), may hold values from -0.125 to 0.125
- w_up: bfloat16 [2048, 16, 1024], P('wide', None, 'narrow'), may hold values from -0.125 to 0.125
- w_down: bfloat16 [2048, 16, 1024], P('wide', None, 'narrow'), may hold values from -1.5 to 1.5
Outputs:
- block_out: bfloat16 [4096, 2048], P('wide', 'narrow')
- grad_tokens: float32 [4096, 2048], P('wide', 'narrow')
- grad_norm_attn: float32 [2048], P('narrow')
- grad_query: float32 [2048, 2048], P('wide', 'narrow')
- grad_key: float32 [2048, 2048], P('wide', 'narrow')
- grad_value: float32 [2048, 2048], P('wide', 'narrow')
- grad_norm_query: float32 [2048], P('narrow')
- grad_norm_key: float32 [2048], P('narrow')
- grad_out: float32 [2048, 2048], P('wide', 'narrow')
- grad_norm_ffn: float32 [2048], P('narrow')
- grad_router: float32 [2048, 16], replicated
- grad_gate: float32 [2048, 16, 1024], P('wide', None, 'narrow')
- grad_up: float32 [2048, 16, 1024], P('wide', None, 'narrow')
- grad_down: float32 [2048, 16, 1024], P('wide', None, 'narrow')
Inputs may be any that keep to these rules, and one draw needn't show every extreme that they name: `block_ids`: block numbers never fall along a sequence; each block has 1 to 256 tokens and some block exactly 256. `routes`: each row names 8 different experts; among the tokens of one sequence no expert is named more than 272 times, a bound that some block reaches.
All inputs are finite; a program needn't handle non-finite values.
Results may differ from a plain program's by a relative error of at most 0.025.
Values may be sent and summed in bfloat16 or wider, within the bound.
No kernel may reach another device: no remote copies, remote signals or barrier semaphores. Data moves between devices by JAX's collectives and lax.ppermute only.
A program may use at most 384 MiB of HBM per device.

v0:
```python
import jax
import jax.numpy as jnp
from jax import lax
from jax.sharding import PartitionSpec as P

HD = 128
EXPERTS = 16
TOP = 8
CAP = 272
EPS = 1e-05
query_rows = 512


def rms_scale(values, scales):
    return values * lax.rsqrt(jnp.mean(values * values, axis=-1, keepdims=True) + EPS) * scales


def rope_tables(length, head_dim):
    exponent = jnp.arange(0, head_dim, 2, dtype=jnp.float32) / head_dim
    angles = jnp.arange(length, dtype=jnp.float32)[:, None] * (10000.0 ** (-exponent))[None, :]
    angles = jnp.concatenate([angles, angles], axis=-1)
    return (jnp.cos(angles)[:, None, :], jnp.sin(angles)[:, None, :])


def rotate_half(values, cosines, sine_table):
    middle = values.shape[-1] // 2
    turned = jnp.concatenate([-values[..., middle:], values[..., :middle]], axis=-1)
    return values * cosines + turned * sine_table


def slot_tables(routes, experts, capacity):
    token_count, top_count = routes.shape
    flat_routes = routes.reshape(-1)
    onehot = (flat_routes[:, None] == jnp.arange(experts, dtype=jnp.int32)[None, :]).astype(
        jnp.int32
    )
    earlier = jnp.cumsum(onehot, axis=0) - onehot
    within = jnp.sum(earlier * onehot, axis=1)
    destination = flat_routes * capacity + within
    pair_ids = jnp.arange(token_count * top_count, dtype=jnp.int32)
    owners = (
        jnp.full((experts * capacity,), token_count * top_count, jnp.int32)
        .at[destination]
        .set(pair_ids)
    )
    return (destination.reshape(token_count, top_count), owners)


def swiglu(gate_in, up_in):
    return jax.nn.silu(gate_in) * up_in


def per_device(
    tokens,
    cotangent,
    block_ids,
    routes,
    norm_attn,
    w_query,
    w_key,
    w_value,
    norm_query,
    norm_key,
    w_out,
    norm_ffn,
    w_router,
    w_gate,
    w_up,
    w_down,
):
    lane_index = lax.axis_index("narrow")
    rows_full, cot_full, gain_attn, gain_ffn = (
        lax.all_gather(tokens, "narrow", axis=1, tiled=True),
        lax.all_gather(cotangent, "narrow", axis=1, tiled=True),
        lax.all_gather(norm_attn, "narrow", axis=0, tiled=True),
        lax.all_gather(norm_ffn, "narrow", axis=0, tiled=True),
    )
    length, model_width = rows_full.shape
    head_cols = w_query.shape[1]
    heads_here = head_cols // HD
    score_scale = HD ** (-0.5)
    rows_float = rows_full.astype(jnp.float32)
    cot_float = cot_full.astype(jnp.float32)
    attn_gain = gain_attn.astype(jnp.float32)
    ffn_gain = gain_ffn.astype(jnp.float32)
    normed = rms_scale(rows_float, attn_gain).astype(jnp.bfloat16)
    query_full, key_full, value_full = (
        lax.all_gather(w_query, "wide", axis=0, tiled=True),
        lax.all_gather(w_key, "wide", axis=0, tiled=True),
        lax.all_gather(w_value, "wide", axis=0, tiled=True),
    )
    query_raw = jnp.dot(normed, query_full, preferred_element_type=jnp.float32)
    key_raw = jnp.dot(normed, key_full, preferred_element_type=jnp.float32)
    value_raw = jnp.dot(normed, value_full, preferred_element_type=jnp.float32)
    square_query, square_key = lax.psum(
        (jnp.sum(query_raw * query_raw, axis=1), jnp.sum(key_raw * key_raw, axis=1)), "narrow"
    )
    query_scale = lax.rsqrt(square_query / model_width + EPS)[:, None]
    key_scale = lax.rsqrt(square_key / model_width + EPS)[:, None]
    query_gain = norm_query.astype(jnp.float32)
    key_gain = norm_key.astype(jnp.float32)
    cosines, sine_table = rope_tables(length, HD)
    query_normed = query_raw * query_scale * query_gain
    key_normed = key_raw * key_scale * key_gain

    def rotate_both(query_in, key_in):
        return (
            rotate_half(query_in.reshape(length, heads_here, HD), cosines, sine_table),
            rotate_half(key_in.reshape(length, heads_here, HD), cosines, sine_table),
        )

    (query_rot, key_rot), rotate_pull = jax.vjp(rotate_both, query_normed, key_normed)
    query_bf = query_rot.astype(jnp.bfloat16)
    key_bf = key_rot.astype(jnp.bfloat16)
    value_bf = value_raw.astype(jnp.bfloat16).reshape(length, heads_here, HD)
    seq_blocks = block_ids[0]
    step_rows = min(query_rows, length)

    def block_scores(offset):
        scores = (
            jnp.einsum("qhd,khd->hqk", query_bf, key_bf, preferred_element_type=jnp.float32)
            * score_scale
        )
        allowed = seq_blocks[None, :] <= seq_blocks[offset : offset + step_rows, None]
        return jnp.where(allowed[None], scores, -1e30)

    offset = 0
    scores = block_scores(offset)
    highest = jnp.max(scores, axis=-1, keepdims=True)
    shifted = jnp.exp(scores - highest)
    totals = jnp.sum(shifted, axis=-1, keepdims=True)
    attn_probs = (shifted / totals).astype(jnp.bfloat16)
    attended_parts = jnp.einsum(
        "hqk,khd->qhd", attn_probs, value_bf, preferred_element_type=jnp.float32
    ).astype(jnp.bfloat16)
    total_parts = highest + jnp.log(totals)
    attended = attended_parts.reshape(length, head_cols)
    out_full = lax.all_gather(w_out, "wide", axis=0, tiled=True)
    out_partial = jnp.einsum("td,cd->tc", attended, out_full, preferred_element_type=jnp.float32)
    residual = rows_float + lax.psum(out_partial, "narrow")
    ffn_in = rms_scale(residual, ffn_gain).astype(jnp.bfloat16)
    logits = jnp.dot(ffn_in, w_router, preferred_element_type=jnp.float32)

    def route_gates(logit_values):
        return jnp.take_along_axis(jax.nn.softmax(logit_values, axis=-1), routes, axis=1)

    gate_values, gate_pull = jax.vjp(route_gates, logits)
    destination, owners = slot_tables(routes, EXPERTS, CAP)
    slot_tokens = owners // TOP
    slot_gates = jnp.concatenate([gate_values.reshape(-1), jnp.zeros((1,), jnp.float32)], axis=0)[
        owners
    ]
    padded_in = jnp.concatenate([ffn_in, jnp.zeros((1, model_width), jnp.bfloat16)], axis=0)
    expert_rows = padded_in[slot_tokens].reshape(EXPERTS, CAP, model_width)
    padded_cot = jnp.concatenate([cot_float, jnp.zeros((1, model_width), jnp.float32)], axis=0)
    slot_cot = padded_cot[slot_tokens]
    gate_full, up_full = (
        lax.all_gather(w_gate, "wide", axis=0, tiled=True),
        lax.all_gather(w_up, "wide", axis=0, tiled=True),
    )
    gate_pre = jnp.einsum(
        "ecd,def->ecf", expert_rows, gate_full, preferred_element_type=jnp.float32
    )
    up_pre = jnp.einsum("ecd,def->ecf", expert_rows, up_full, preferred_element_type=jnp.float32)
    hidden_float, swiglu_pull = jax.vjp(swiglu, gate_pre, up_pre)
    hidden_bf = hidden_float.astype(jnp.bfloat16)
    down_full = lax.all_gather(w_down, "wide", axis=0, tiled=True)
    expert_out = jnp.einsum(
        "ecf,def->ecd", hidden_bf, down_full, preferred_element_type=jnp.float32
    ).reshape(EXPERTS * CAP, model_width)
    moe_partial = (
        jnp.zeros((length + 1, model_width), jnp.float32)
        .at[slot_tokens]
        .add(slot_gates[:, None] * expert_out)[:length]
    )
    slot_dots = jnp.concatenate(
        [jnp.sum(expert_out * slot_cot, axis=1), jnp.zeros((1,), jnp.float32)], axis=0
    )
    dots_partial = slot_dots[destination]
    expert_cot = (
        (slot_gates[:, None] * slot_cot).astype(jnp.bfloat16).reshape(EXPERTS, CAP, model_width)
    )
    hidden_grad = jnp.einsum(
        "ecd,def->ecf", expert_cot, down_full, preferred_element_type=jnp.float32
    )
    gate_grad, up_grad = swiglu_pull(hidden_grad)
    gate_grad_bf = gate_grad.astype(jnp.bfloat16)
    up_grad_bf = up_grad.astype(jnp.bfloat16)
    rows_grad = jnp.einsum(
        "ecf,def->ecd", gate_grad_bf, gate_full, preferred_element_type=jnp.float32
    ) + jnp.einsum("ecf,def->ecd", up_grad_bf, up_full, preferred_element_type=jnp.float32)
    input_partial = (
        jnp.zeros((length + 1, model_width), jnp.float32)
        .at[slot_tokens]
        .add(rows_grad.reshape(EXPERTS * CAP, model_width))[:length]
    )
    pair_dots, input_sum, moe_sum = (
        lax.psum(dots_partial.astype(jnp.bfloat16), "narrow").astype(jnp.float32),
        lax.psum(input_partial.astype(jnp.bfloat16), "narrow").astype(jnp.float32),
        lax.psum(moe_partial.astype(jnp.bfloat16), "narrow").astype(jnp.float32),
    )
    block_rows = residual + moe_sum
    block_out = lax.dynamic_slice_in_dim(block_rows, lane_index * head_cols, head_cols, 1).astype(
        jnp.bfloat16
    )
    logit_grad = gate_pull(pair_dots)[0].astype(jnp.bfloat16)
    ffn_grad = input_sum + jnp.einsum(
        "te,de->td", logit_grad, w_router, preferred_element_type=jnp.float32
    )
    router_grad = jnp.einsum("td,te->de", ffn_in, logit_grad, preferred_element_type=jnp.float32)
    _, ffn_norm_pull = jax.vjp(rms_scale, residual, ffn_gain)
    residual_norm_grad, ffn_gain_grad = ffn_norm_pull(ffn_grad)
    residual_grad = cot_float + residual_norm_grad
    out_cot = residual_grad.astype(jnp.bfloat16)
    attended_grad = (
        jnp.einsum("tc,cd->td", out_cot, out_full, preferred_element_type=jnp.float32)
        .astype(jnp.bfloat16)
        .reshape(length, heads_here, HD)
    )
    offset = 0
    scores = block_scores(offset)
    attn_probs = jnp.exp(scores - total_parts)
    prob_grad = jnp.einsum(
        "qhd,khd->hqk", attended_grad, value_bf, preferred_element_type=jnp.float32
    )
    centre = jnp.sum(attn_probs * prob_grad, axis=-1, keepdims=True)
    score_grad = (attn_probs * (prob_grad - centre)).astype(jnp.bfloat16)
    query_grad_parts = (
        jnp.einsum("hqk,khd->qhd", score_grad, key_bf, preferred_element_type=jnp.float32)
        * score_scale
    )
    key_grad = (
        jnp.einsum("hqk,qhd->khd", score_grad, query_bf, preferred_element_type=jnp.float32)
        * score_scale
    )
    value_grad = jnp.einsum(
        "hqk,qhd->khd",
        attn_probs.astype(jnp.bfloat16),
        attended_grad,
        preferred_element_type=jnp.float32,
    )
    query_normed_grad, key_normed_grad = rotate_pull((query_grad_parts, key_grad))
    dot_query, dot_key = lax.psum(
        (
            jnp.sum(query_gain * query_normed_grad * query_raw, axis=1),
            jnp.sum(key_gain * key_normed_grad * key_raw, axis=1),
        ),
        "narrow",
    )
    query_pre_grad = (
        query_scale * query_gain * query_normed_grad
        - query_raw * query_scale**3 * dot_query[:, None] / model_width
    )
    key_pre_grad = (
        key_scale * key_gain * key_normed_grad
        - key_raw * key_scale**3 * dot_key[:, None] / model_width
    )
    query_gain_grad = jnp.sum(query_normed_grad * query_raw * query_scale, axis=0)
    key_gain_grad = jnp.sum(key_normed_grad * key_raw * key_scale, axis=0)
    query_grad_bf = query_pre_grad.astype(jnp.bfloat16)
    key_grad_bf = key_pre_grad.astype(jnp.bfloat16)
    value_grad_bf = value_grad.reshape(length, head_cols).astype(jnp.bfloat16)
    normed_partial = jnp.einsum(
        "tc,dc->td", query_grad_bf, query_full, preferred_element_type=jnp.float32
    )
    normed_partial = normed_partial + jnp.einsum(
        "tc,dc->td", key_grad_bf, key_full, preferred_element_type=jnp.float32
    )
    normed_partial = normed_partial + jnp.einsum(
        "tc,dc->td", value_grad_bf, value_full, preferred_element_type=jnp.float32
    )
    normed_grad = lax.psum(normed_partial.astype(jnp.bfloat16), "narrow").astype(jnp.float32)
    _, attn_norm_pull = jax.vjp(rms_scale, rows_float, attn_gain)
    rows_norm_grad, attn_gain_grad = attn_norm_pull(normed_grad)
    grad_tokens = lax.dynamic_slice_in_dim(
        residual_grad + rows_norm_grad, lane_index * head_cols, head_cols, 1
    )
    small_terms = (
        router_grad,
        lax.dynamic_slice_in_dim(attn_gain_grad, lane_index * head_cols, head_cols, 0),
        lax.dynamic_slice_in_dim(ffn_gain_grad, lane_index * head_cols, head_cols, 0),
        query_gain_grad,
        key_gain_grad,
    )
    grad_router, grad_norm_attn, grad_norm_ffn, grad_norm_query, grad_norm_key = (
        lax.psum(small_terms[0].astype(jnp.bfloat16), "wide").astype(jnp.float32),
        lax.psum(small_terms[1].astype(jnp.bfloat16), "wide").astype(jnp.float32),
        lax.psum(small_terms[2].astype(jnp.bfloat16), "wide").astype(jnp.float32),
        lax.psum(small_terms[3].astype(jnp.bfloat16), "wide").astype(jnp.float32),
        lax.psum(small_terms[4].astype(jnp.bfloat16), "wide").astype(jnp.float32),
    )
    query_term = jnp.einsum("tc,tf->cf", normed, query_grad_bf, preferred_element_type=jnp.float32)
    key_term = jnp.einsum("tc,tf->cf", normed, key_grad_bf, preferred_element_type=jnp.float32)
    value_term = jnp.einsum("tc,tf->cf", normed, value_grad_bf, preferred_element_type=jnp.float32)
    out_term = jnp.einsum("tc,tf->cf", out_cot, attended, preferred_element_type=jnp.float32)
    gate_term = jnp.einsum(
        "ecd,ecf->def", expert_rows, gate_grad_bf, preferred_element_type=jnp.float32
    )
    up_term = jnp.einsum(
        "ecd,ecf->def", expert_rows, up_grad_bf, preferred_element_type=jnp.float32
    )
    down_term = jnp.einsum(
        "ecd,ecf->def", expert_cot, hidden_bf, preferred_element_type=jnp.float32
    )
    gate_term, up_term, down_term = (gate_term, up_term, down_term)
    grad_query, grad_key, grad_value, grad_out, grad_gate, grad_up, grad_down = (
        lax.psum_scatter(
            query_term.astype(jnp.bfloat16), "wide", scatter_dimension=0, tiled=True
        ).astype(jnp.float32),
        lax.psum_scatter(
            key_term.astype(jnp.bfloat16), "wide", scatter_dimension=0, tiled=True
        ).astype(jnp.float32),
        lax.psum_scatter(
            value_term.astype(jnp.bfloat16), "wide", scatter_dimension=0, tiled=True
        ).astype(jnp.float32),
        lax.psum_scatter(
            out_term.astype(jnp.bfloat16), "wide", scatter_dimension=0, tiled=True
        ).astype(jnp.float32),
        lax.psum_scatter(
            gate_term.astype(jnp.bfloat16), "wide", scatter_dimension=0, tiled=True
        ).astype(jnp.float32),
        lax.psum_scatter(
            up_term.astype(jnp.bfloat16), "wide", scatter_dimension=0, tiled=True
        ).astype(jnp.float32),
        lax.psum_scatter(
            down_term.astype(jnp.bfloat16), "wide", scatter_dimension=0, tiled=True
        ).astype(jnp.float32),
    )
    return (
        block_out,
        grad_tokens,
        grad_norm_attn,
        grad_query,
        grad_key,
        grad_value,
        grad_norm_query,
        grad_norm_key,
        grad_out,
        grad_norm_ffn,
        grad_router,
        grad_gate,
        grad_up,
        grad_down,
    )


def solution(mesh):
    placed = (
        P("wide", "narrow"),
        P("wide", "narrow"),
        P("wide", None),
        P("wide", None),
        P("narrow"),
        P("wide", "narrow"),
        P("wide", "narrow"),
        P("wide", "narrow"),
        P("narrow"),
        P("narrow"),
        P("wide", "narrow"),
        P("narrow"),
        P(),
        P("wide", None, "narrow"),
        P("wide", None, "narrow"),
        P("wide", None, "narrow"),
    )
    return jax.shard_map(
        per_device,
        mesh=mesh,
        in_specs=placed,
        out_specs=(
            P("wide", "narrow"),
            P("wide", "narrow"),
            P("narrow"),
            P("wide", "narrow"),
            P("wide", "narrow"),
            P("wide", "narrow"),
            P("narrow"),
            P("narrow"),
            P("wide", "narrow"),
            P("narrow"),
            P(),
            P("wide", None, "narrow"),
            P("wide", None, "narrow"),
            P("wide", None, "narrow"),
        ),
        check_vma=False,
    )
```

profile of v0, /device:TPU:0, one launch (start us, length us, event | category | flops | bytes accessed | tf_op | source)
XLA Modules:
  0.0 2680.0 jit_solution(7671028160317145200)
XLA Ops:
  37.0 49.3 %all-gather.16.cloned.1.call-done = bf16[2048,512]{1,0:T(8,128)(2,1)} async-done(((bf16[256,512]{1,0:T(8,128)(2,1)}), bf16[2048,512]{1,0:T(8,128)(2,1)}) %all-gather.16.cloned.1.call-update) | async-done | bytes 2097168 | tf_op jit(solution)/shard_map/all_gather | solution.py:88
  90.1 46.2 %all-gather.18.cloned.1.call-done = bf16[2048,512]{1,0:T(8,128)(2,1)} async-done(((bf16[256,512]{1,0:T(8,128)(2,1)}), bf16[2048,512]{1,0:T(8,128)(2,1)}) %all-gather.18.cloned.1.call-update) | async-done | bytes 2097168 | tf_op jit(solution)/shard_map/all_gather | solution.py:89
  152.6 33.5 %all-gather.14.cloned.1.call-done = bf16[2048,512]{1,0:T(8,128)(2,1)} async-done(((bf16[256,512]{1,0:T(8,128)(2,1)}), bf16[2048,512]{1,0:T(8,128)(2,1)}) %all-gather.14.cloned.1.call-update) | async-done | bytes 2097168 | tf_op jit(solution)/shard_map/all_gather | solution.py:90
  191.0 44.9 %all-gather.20.cloned.1.call-done = bf16[2048,512]{1,0:T(8,128)(2,1)} async-done(((bf16[256,512]{1,0:T(8,128)(2,1)}), bf16[2048,512]{1,0:T(8,128)(2,1)}) %all-gather.20.cloned.1.call-update) | async-done | bytes 2097168 | tf_op jit(solution)/shard_map/all_gather | solution.py:138
  287.1 34.3 %gather_fusion.2 = f32[4352,2048]{1,0:T(8,128)} fusion(f32[513,2048]{1,0:T(8,128)} %concatenate.34, s32[5120]{0:T(1024)S(1)} %pad_clamp_fusion), kind=kCustom, calls=%fused_computation.2 | custom fusion | bytes 71320576 | tf_op jit(solution)/shard_map/gather | solution.py:156
  322.0 24.9 all-reduce.15.cloned.1.call-done
  352.5 33.0 %gather_fusion.4 = f32[4096]{0:T(1024)S(1)} fusion(f32[512,16]{0,1:T(8,128)S(1)} %fusion.49, s32[4096]{0:T(1024)S(1)} %reshape.331), kind=kCustom, calls=%fused_computation.4 | custom fusion | bytes 65536 | tf_op jit(solution)/shard_map/jvp(jit(take_along_axis))/gather | solution.py:145
  386.2 22.8 gather_fusion
  429.2 147.9 %all-gather.22.cloned.1.call-done = bf16[2048,16,256]{2,0,1:T(8,128)(2,1)} async-done(((bf16[256,16,256]{2,0,1:T(8,128)(2,1)}), bf16[2048,16,256]{2,0,1:T(8,128)(2,1)}) %all-gather.22.cloned.1.call-update) | async-done | bytes 16777232 | tf_op jit(solution)/shard_map/all_gather | solution.py:158
  593.7 211.7 %all-gather.24.cloned.1.call-done = bf16[2048,16,256]{2,0,1:T(8,128)(2,1)} async-done(((bf16[256,16,256]{2,0,1:T(8,128)(2,1)}), bf16[2048,16,256]{2,0,1:T(8,128)(2,1)}) %all-gather.24.cloned.1.call-update) | async-done | bytes 16777232 | tf_op jit(solution)/shard_map/all_gather | solution.py:159
  821.9 211.5 %all-gather.26.cloned.1.call-done = bf16[2048,16,256]{2,0,1:T(8,128)(2,1)} async-done(((bf16[256,16,256]{2,0,1:T(8,128)(2,1)}), bf16[2048,16,256]{2,0,1:T(8,128)(2,1)}) %all-gather.26.cloned.1.call-update) | async-done | bytes 16777232 | tf_op jit(solution)/shard_map/all_gather | solution.py:167
  1033.4 34.2 %multiply_convert_fusion.3 = (bf16[16,272,256]{2,1,0:T(8,128)(2,1)}, bf16[16,272,256]{2,1,0:T(8,128)(2,1)S(1)}, bf16[16,272,256]{2,1,0:T(8,128)(2,1)}) fusion(f32[16,272,256]{2,1,0:T(8,128)} %fusion.67, f32[16,272,256]{2,1,0:T(8,128)} %fusion.68, bf16[2048,16,256]{2,0,1:T(8,128)(2,1)} %all-gather.26.cloned.1.call-done, f32[16,272,2048]{2,1,0:T(8,128)} %bitcast.142, ...), kind=kOutput, calls=%fused_computation.24 | convolution fusion | flops 4599054336 | bytes 68043776 | tf_op jit(solution)/shard_map/ecd,def->ecf/dot_general | solution.py:183
  1067.6 25.4 fusion.69
  1093.0 31.1 %convolution_add_fusion = f32[16,272,2048]{2,1,0:T(8,128)} fusion(f32[16,272,2048]{2,1,0:T(8,128)} %fusion.69, bf16[16,272,256]{2,1,0:T(8,128)(2,1)} %get-tuple-element.104, bf16[2048,16,256]{2,0,1:T(8,128)(2,1)} %all-gather.24.cloned.1.call-done), kind=kOutput, calls=%fused_computation.12 | convolution fusion | flops 4572315648 | bytes 90308608 | tf_op jit(solution)/shard_map/ecf,def->ecd/dot_general | solution.py:191
  1124.1 60.5 %scatter_custom_fusion.2 = f32[513,2048]{1,0:T(8,128)} fusion(s32[4352]{0:T(1024)} %copy-done.52, f32[4352,2048]{1,0:T(8,128)} %bitcast.149, f32[]{:T(128)} %constant.32.clone.1), kind=kCustom, calls=%fused_computation.56 | custom fusion | flops 8912896 | bytes 4203008 | tf_op jit(solution)/shard_map/scatter-add | solution.py:195
  1188.8 31.0 %multiply_reduce_fusion = (bf16[16,272]{1,0:T(8,128)(2,1)S(1)}, f32[16,272,2048]{2,1,0:T(8,128)}) fusion(f32[16,272,2048]{2,1,0:T(8,128)} %bitcast.143, bf16[16,272,256]{2,1,0:T(8,128)(2,1)S(1)} %copy-done.16, bf16[2048,16,256]{2,0,1:T(8,128)(2,1)} %all-gather.26.cloned.1.call-done), kind=kOutput, calls=%fused_computation.10 | convolution fusion | flops 4581224448 | bytes 90317312 | tf_op jit(solution)/shard_map/ecf,def->ecd/dot_general | solution.py:168
  1219.8 26.7 bitcast_multiply_fusion
  1246.7 25.6 gather_fusion.3
  1285.0 22.1 scatter_custom_fusion.3
  1307.2 60.9 %scatter_custom_fusion.1 = f32[513,2048]{1,0:T(8,128)} fusion(s32[4352]{0:T(1024)} %copy-done.52, f32[4352,2048]{1,0:T(8,128)} %bitcast_multiply_fusion, f32[]{:T(128)} %constant.32.clone.1), kind=kCustom, calls=%fused_computation.58 | custom fusion | flops 8912896 | bytes 4203008 | tf_op jit(solution)/shard_map/scatter-add | solution.py:174
  1420.0 20.4 convert_bitcast_fusion
  1440.5 18.9 convert_bitcast_fusion.2
  1459.7 19.0 convert_bitcast_fusion.1
  1482.9 44.9 %all-reduce.21.cloned.1.call-done = (bf16[512,2048]{1,0:T(8,128)(2,1)}, bf16[512,2048]{1,0:T(8,128)(2,1)}) async-done(((bf16[512,2048]{1,0:T(8,128)(2,1)}, bf16[512,2048]{1,0:T(8,128)(2,1)}), (bf16[512,2048]{1,0:T(8,128)(2,1)}, bf16[512,2048]{1,0:T(8,128)(2,1)})) %all-reduce.21.cloned.1.call-update) | async-done | bytes 4194320 | tf_op jit(solution)/shard_map/psum | solution.py:200
  1533.1 21.6 all-reduce.8
  1562.4 36.9 %reduce-scatter.12.cloned.1.call-done = bf16[256,512]{1,0:T(8,128)(2,1)} async-done(((bf16[2048,512]{1,0:T(8,128)(2,1)}), bf16[256,512]{1,0:T(8,128)(2,1)}) %reduce-scatter.12.cloned.1.call-update) | async-done | bytes 262160 | tf_op jit(solution)/shard_map/reduce_scatter | solution.py:313
  1601.1 68.6 %reduce-scatter.10.cloned.1.call-done = bf16[256,512]{1,0:T(8,128)(2,1)} async-done(((bf16[2048,512]{1,0:T(8,128)(2,1)}), bf16[256,512]{1,0:T(8,128)(2,1)}) %reduce-scatter.10.cloned.1.call-update) | async-done | bytes 262160 | tf_op jit(solution)/shard_map/reduce_scatter | solution.py:310
  1671.5 68.8 %reduce-scatter.8.cloned.1.call-done = bf16[256,512]{1,0:T(8,128)(2,1)} async-done(((bf16[2048,512]{1,0:T(8,128)(2,1)}), bf16[256,512]{1,0:T(8,128)(2,1)}) %reduce-scatter.8.cloned.1.call-update) | async-done | bytes 262160 | tf_op jit(solution)/shard_map/reduce_scatter | solution.py:307
  1742.1 68.6 %reduce-scatter.14.cloned.1.call-done = bf16[256,512]{1,0:T(8,128)(2,1)} async-done(((bf16[2048,512]{1,0:T(8,128)(2,1)}), bf16[256,512]{1,0:T(8,128)(2,1)}) %reduce-scatter.14.cloned.1.call-update) | async-done | bytes 262160 | tf_op jit(solution)/shard_map/reduce_scatter | solution.py:316
  1812.5 284.1 %reduce-scatter.20.cloned.1.call-done = bf16[256,16,256]{0,2,1:T(8,128)(2,1)} async-done(((bf16[2048,16,256]{0,2,1:T(8,128)(2,1)}), bf16[256,16,256]{0,2,1:T(8,128)(2,1)}) %reduce-scatter.20.cloned.1.call-update) | async-done | bytes 2097168 | tf_op jit(solution)/shard_map/reduce_scatter | solution.py:325
  2101.3 280.9 %reduce-scatter.16.cloned.1.call-done = bf16[256,16,256]{0,2,1:T(8,128)(2,1)} async-done(((bf16[2048,16,256]{0,2,1:T(8,128)(2,1)}), bf16[256,16,256]{0,2,1:T(8,128)(2,1)}) %reduce-scatter.16.cloned.1.call-update) | async-done | bytes 2097168 | tf_op jit(solution)/shard_map/reduce_scatter | solution.py:319
  2387.0 281.0 %reduce-scatter.18.cloned.1.call-done = bf16[256,16,256]{0,2,1:T(8,128)(2,1)} async-done(((bf16[2048,16,256]{0,2,1:T(8,128)(2,1)}), bf16[256,16,256]{0,2,1:T(8,128)(2,1)}) %reduce-scatter.18.cloned.1.call-update) | async-done | bytes 2097168 | tf_op jit(solution)/shard_map/reduce_scatter | solution.py:322
  (344 shorter events, 272.8 us)
Async XLA Ops:
  7.2 343.0 %copy-start = (bf16[2048,16]{0,1:T(8,128)(2,1)S(1)}, bf16[2048,16]{0,1:T(8,128)(2,1)}, u32[]{:S(2)}) copy-start(bf16[2048,16]{0,1:T(8,128)(2,1)} %param.28) | copy-start | bytes 196612
  7.2 27.7 %all-gather.12.cloned.1.call-start = ((), (), s32[]{:S(2)}) async-start(), calls=%async_computation.7 | async-start | bytes 2621440 | tf_op jit(solution)/shard_map/all_gather | solution.py:73
  7.9 78.4 %all-gather.16.cloned.1.call-start = ((), (), s32[]{:S(2)}) async-start(), calls=%async_computation.9 | async-start | bytes 2359296 | tf_op jit(solution)/shard_map/all_gather | solution.py:88
  8.7 127.6 %all-gather.18.cloned.1.call-start = ((), (), s32[]{:S(2)}) async-start(), calls=%async_computation.10 | async-start | bytes 2359296 | tf_op jit(solution)/shard_map/all_gather | solution.py:89
  9.4 176.7 %all-gather.14.cloned.1.call-start = ((), (), s32[]{:S(2)}) async-start(), calls=%async_computation.8 | async-start | bytes 2359296 | tf_op jit(solution)/shard_map/all_gather | solution.py:90
  10.0 225.9 %all-gather.20.cloned.1.call-start = ((), (), s32[]{:S(2)}) async-start(), calls=%async_computation.11 | async-start | bytes 2359296 | tf_op jit(solution)/shard_map/all_gather | solution.py:138
  10.6 272.3 %all-gather.28.cloned.1.call-start = ((), (), s32[]{:S(2)}) async-start(), calls=%async_computation.16 | async-start | bytes 2621440 | tf_op jit(solution)/shard_map/all_gather | solution.py:74
  11.2 335.8 %all-reduce.15.cloned.1.call-start = ((), (), s32[]{:S(2)}) async-start(), calls=%async_computation.12 | async-start | bytes 8388608 | tf_op jit(solution)/shard_map/psum | solution.py:140
  18.0 168.1 %copy-start.65 = (f32[4,1,512]{2,1,0:T(1,128)}, f32[4,1,512]{2,1,0:T(1,128)S(1)}, u32[]{:S(2)}) copy-start(f32[4,1,512]{2,1,0:T(1,128)S(1)} %convert_element_type.261) | copy-start | bytes 24580
  18.7 127.8 %copy-start.57 = (f32[512]{0:T(512)}, f32[512]{0:T(512)S(1)}, u32[]{:S(2)}) copy-start(f32[512]{0:T(512)S(1)} %convert_element_type.200) | copy-start | bytes 6148
  19.4 127.4 %copy-start.59 = (f32[512]{0:T(512)}, f32[512]{0:T(512)S(1)}, u32[]{:S(2)}) copy-start(f32[512]{0:T(512)S(1)} %convert_element_type.202) | copy-start | bytes 6148
  37.0 149.1 %copy-start.71 = (f32[512]{0:T(512)}, f32[512]{0:T(512)S(1)}, u32[]{:S(2)}) copy-start(f32[512]{0:T(512)S(1)} %fusion.58) | copy-start | bytes 6148
  240.8 336.3 %all-gather.22.cloned.1.call-start = ((), (), s32[]{:S(2)}) async-start(), calls=%async_computation.13 | async-start | bytes 18874368 | tf_op jit(solution)/shard_map/all_gather | solution.py:158
  244.7 560.6 %all-gather.24.cloned.1.call-start = ((), (), s32[]{:S(2)}) async-start(), calls=%async_computation.14 | async-start | bytes 18874368 | tf_op jit(solution)/shard_map/all_gather | solution.py:159
  248.6 784.8 %all-gather.26.cloned.1.call-start = ((), (), s32[]{:S(2)}) async-start(), calls=%async_computation.15 | async-start | bytes 18874368 | tf_op jit(solution)/shard_map/all_gather | solution.py:167
  252.4 1121.1 %all-reduce.17.cloned.1.call-start = ((), (), s32[]{:S(2)}) async-start(), calls=%async_computation.17 | async-start | bytes 4194304 | tf_op jit(solution)/shard_map/psum | solution.py:199
  258.1 91.7 %copy-start.47 = (f32[4,1,512]{2,1,0:T(1,128)}, f32[4,1,512]{2,1,0:T(1,128)S(1)}, u32[]{:S(2)}) copy-start(f32[4,1,512]{2,1,0:T(1,128)S(1)} %convert_element_type.262) | copy-start | bytes 24580
  352.5 76.2 %copy-start.55 = (f32[512]{0:T(512)}, f32[512]{0:T(512)S(1)}, u32[]{:S(2)}) copy-start(f32[512]{0:T(512)S(1)} %fusion.50) | copy-start | bytes 6148
  409.7 623.8 %copy-start.49 = (f32[16,272]{1,0:T(8,128)}, f32[16,272]{1,0:T(8,128)S(1)}, u32[]{:S(2)}) copy-start(f32[16,272]{1,0:T(8,128)S(1)} %mul.486) | copy-start | bytes 52228
  1188.7 292.6 %all-reduce.19.cloned.1.call-start = ((), (), s32[]{:S(2)}) async-start(), calls=%async_computation.22 | async-start | bytes 131072 | tf_op jit(solution)/shard_map/psum | solution.py:286
  1246.7 60.5 %copy-start.39 = (f32[512,16]{0,1:T(8,128)S(1)}, f32[512,16]{0,1:T(8,128)}, u32[]{:S(2)}) copy-start(f32[512,16]{0,1:T(8,128)} %copy-done.38) | copy-start | bytes 98308
  1246.7 60.5 %copy-start.54 = (f32[512]{0:T(512)S(1)}, f32[512]{0:T(512)}, u32[]{:S(2)}) copy-start(f32[512]{0:T(512)} %copy-done.53) | copy-start | bytes 6148
  1307.2 64.8 %copy-start.56 = (f32[512]{0:T(512)S(1)}, f32[512]{0:T(512)}, u32[]{:S(2)}) copy-start(f32[512]{0:T(512)} %copy-done.55) | copy-start | bytes 6148
  1307.2 64.8 %copy-start.8 = (bf16[512,2048]{1,0:T(8,128)(2,1)S(1)}, bf16[512,2048]{1,0:T(8,128)(2,1)}, u32[]{:S(2)}) copy-start(bf16[512,2048]{1,0:T(8,128)(2,1)} %copy-done.7) | copy-start | bytes 6291460
  1373.1 154.7 %all-reduce.21.cloned.1.call-start = ((), (), s32[]{:S(2)}) async-start(), calls=%async_computation.26 | async-start | bytes 8388608 | tf_op jit(solution)/shard_map/psum | solution.py:200
  1404.6 194.7 %reduce-scatter.12.cloned.1.call-start = ((), (), s32[]{:S(2)}) async-start(), calls=%async_computation.20 | async-start | bytes 2359296 | tf_op jit(solution)/shard_map/reduce_scatter | solution.py:313
  1409.0 260.7 %reduce-scatter.10.cloned.1.call-start = ((), (), s32[]{:S(2)}) async-start(), calls=%async_computation.19 | async-start | bytes 2359296 | tf_op jit(solution)/shard_map/reduce_scatter | solution.py:310
  1411.9 328.3 %reduce-scatter.8.cloned.1.call-start = ((), (), s32[]{:S(2)}) async-start(), calls=%async_computation.18 | async-start | bytes 2359296 | tf_op jit(solution)/shard_map/reduce_scatter | solution.py:307
  1414.9 395.8 %reduce-scatter.14.cloned.1.call-start = ((), (), s32[]{:S(2)}) async-start(), calls=%async_computation.21 | async-start | bytes 2359296 | tf_op jit(solution)/shard_map/reduce_scatter | solution.py:316
  1419.7 676.8 %reduce-scatter.20.cloned.1.call-start = ((), (), s32[]{:S(2)}) async-start(), calls=%async_computation.25 | async-start | bytes 18874368 | tf_op jit(solution)/shard_map/reduce_scatter | solution.py:325
  1440.5 941.7 %reduce-scatter.16.cloned.1.call-start = ((), (), s32[]{:S(2)}) async-start(), calls=%async_computation.23 | async-start | bytes 18874368 | tf_op jit(solution)/shard_map/reduce_scatter | solution.py:319
  1459.4 1208.6 %reduce-scatter.18.cloned.1.call-start = ((), (), s32[]{:S(2)}) async-start(), calls=%async_computation.24 | async-start | bytes 18874368 | tf_op jit(solution)/shard_map/reduce_scatter | solution.py:322
  (69 other events, 658.3 us)
Sparse Core Ops, SparseCore 0:
  9.6 25.2 all-gather.11
  37.0 49.2 all-gather.15
  88.5 47.7 all-gather.17
  138.3 47.7 all-gather.13
  188.1 47.7 all-gather.19
  237.3 21.0 all-gather.27
  261.4 85.5 all-reduce.14
  349.3 227.7 all-gather.21
  579.5 225.7 all-gather.23
  807.6 225.7 all-gather.25
  1188.8 49.5 all-reduce.16
  1373.2 66.4 all-reduce.18
  1442.1 85.6 all-reduce.20
  1531.5 67.7 reduce-scatter.11
  1603.1 66.5 reduce-scatter.9
  1673.5 66.7 reduce-scatter.7
  1744.1 66.5 reduce-scatter.13
  1814.8 281.7 reduce-scatter.19
  2100.3 281.8 reduce-scatter.15
  2386.3 281.6 reduce-scatter.17
where the time goes:
time: 2690 us; the launch traced here: 2680 us
  waiting for transfers between devices  1920 us (71%)
  matrix products  261 us (10%)
  other arithmetic  221 us (8%)
  local copies, waits for them, and re-layouts  205 us (8%)
  blocking collectives  56.7 us (2%)
    reduce_scatter x1, waiting for transfers between devices, per_device(): lax.psum_scatter(down_term.astype(jnp.bfloat16), 'wide', scatter_dimensio...  284 us
    reduce_scatter x1, waiting for transfers between devices, per_device(): lax.psum_scatter(up_term.astype(jnp.bfloat16), 'wide', scatter_dimension=...  281 us
    reduce_scatter x1, waiting for transfers between devices, per_device(): lax.psum_scatter(gate_term.astype(jnp.bfloat16), 'wide', scatter_dimensio...  281 us
    all_gather x1, waiting for transfers between devices, per_device(): lax.all_gather(w_up, 'wide', axis=0, tiled=True)  212 us
    all_gather x1, waiting for transfers between devices, per_device(): down_full = lax.all_gather(w_down, 'wide', axis=0, tiled=True)  211 us
    all_gather x1, waiting for transfers between devices, per_device(): lax.all_gather(w_gate, 'wide', axis=0, tiled=True)  148 us
    reduce_scatter x1, waiting for transfers between devices, per_device(): lax.psum_scatter(query_term.astype(jnp.bfloat16), 'wide', scatter_dimensi...  68.8 us
    reduce_scatter x1, waiting for transfers between devices, per_device(): lax.psum_scatter(key_term.astype(jnp.bfloat16), 'wide', scatter_dimension...  68.6 us
  transfers between devices with their start and end apart: 20, of which 17 were waited for; matrix products, arithmetic and copies ran while one was open for 19% of the time, Pallas kernels for 0%

commit v1 on v0

--- a/solution.py
+++ b/solution.py
@@ -164,7 +164,18 @@
     up_pre = jnp.einsum("ecd,def->ecf", expert_rows, up_full, preferred_element_type=jnp.float32)
     hidden_float, swiglu_pull = jax.vjp(swiglu, gate_pre, up_pre)
     hidden_bf = hidden_float.astype(jnp.bfloat16)
-    down_full = lax.all_gather(w_down, "wide", axis=0, tiled=True)
+    t_next, lower, u_next = (jax.lax.axis_size("wide"), jax.lax.axis_index("wide"), w_down.shape[0])
+    small, reply = (w_down, 1)
+    while reply < t_next:
+        small = jnp.concatenate(
+            [
+                small,
+                jax.lax.ppermute(small, "wide", [(q, (q - reply) % t_next) for q in range(t_next)]),
+            ],
+            axis=0,
+        )
+        reply = 2 * reply
+    down_full = jnp.roll(small, shift=lower * u_next, axis=0)
     expert_out = jnp.einsum(
         "ecf,def->ecd", hidden_bf, down_full, preferred_element_type=jnp.float32
     ).reshape(EXPERTS * CAP, model_width)

time: 2690 us -> 2820 us (1.048)
  waiting for transfers between devices: 1920 us -> 2030 us
    ppermute x0 -> x3, waiting for transfers between devices: none -> 689 us  [per_device(): jax.lax.ppermute(small, 'wide', [(q, (q - reply) % t_next) for q in range...]
    all_gather x1 -> x0, waiting for transfers between devices: 211 us -> none  [per_device(): down_full = lax.all_gather(w_down, 'wide', axis=0, tiled=True)]
    all_gather x1, waiting for transfers between devices: 212 us -> 8.53 us  [per_device(): lax.all_gather(w_up, 'wide', axis=0, tiled=True)]
    all_gather x1, waiting for transfers between devices: 148 us -> 0.01 us  [per_device(): lax.all_gather(w_gate, 'wide', axis=0, tiled=True)]
    unnamed x173 -> x187, local copies, waits for them, and re-layouts: 39.2 us -> 60.4 us
  transfers between devices with their start and end apart: 20 -> 22, of which waited for: 17 -> 17; matrix products, arithmetic and copies ran while one was open for 19% -> 19% of each run, Pallas kernels for 0% -> 0%
where the time goes in v1:
time: 2820 us; the launch traced here: 2810 us
  waiting for transfers between devices  2030 us (72%)
  matrix products  240 us (9%)
  local copies, waits for them, and re-layouts  233 us (8%)
  other arithmetic  226 us (8%)
  blocking collectives  57.6 us (2%)
    ppermute x3, waiting for transfers between devices, per_device(): jax.lax.ppermute(small, 'wide', [(q, (q - reply) % t_next) for q in range...  689 us
    reduce_scatter x1, waiting for transfers between devices, per_device(): lax.psum_scatter(down_term.astype(jnp.bfloat16), 'wide', scatter_dimensio...  284 us
    reduce_scatter x1, waiting for transfers between devices, per_device(): lax.psum_scatter(up_term.astype(jnp.bfloat16), 'wide', scatter_dimension=...  281 us
    reduce_scatter x1, waiting for transfers between devices, per_device(): lax.psum_scatter(gate_term.astype(jnp.bfloat16), 'wide', scatter_dimensio...  281 us
    reduce_scatter x1, waiting for transfers between devices, per_device(): lax.psum_scatter(query_term.astype(jnp.bfloat16), 'wide', scatter_dimensi...  68.8 us
    reduce_scatter x1, waiting for transfers between devices, per_device(): lax.psum_scatter(out_term.astype(jnp.bfloat16), 'wide', scatter_dimension...  68.7 us
    reduce_scatter x1, waiting for transfers between devices, per_device(): lax.psum_scatter(key_term.astype(jnp.bfloat16), 'wide', scatter_dimension...  68.6 us
    scatter-add x1, other arithmetic, per_device(): moe_partial = jnp.zeros((length + 1, model_width), jnp.float32).at[slot_t...  60.9 us
  transfers between devices with their start and end apart: 22, of which 17 were waited for; matrix products, arithmetic and copies ran while one was open for 19% of the time, Pallas kernels for 0%

profile of v1, /device:TPU:0, one launch (start us, length us, event | category | flops | bytes accessed | tf_op | source)
XLA Modules:
  0.0 2808.8 jit_solution(3978545217644959428)
XLA Ops:
  37.0 49.3 %all-gather.15.cloned.1.call-done = bf16[2048,512]{1,0:T(8,128)(2,1)} async-done(((bf16[256,512]{1,0:T(8,128)(2,1)}), bf16[2048,512]{1,0:T(8,128)(2,1)}) %all-gather.15.cloned.1.call-update) | async-done | bytes 2097168 | tf_op jit(solution)/shard_map/all_gather | solution.py:88
  90.1 46.2 %all-gather.17.cloned.1.call-done = bf16[2048,512]{1,0:T(8,128)(2,1)} async-done(((bf16[256,512]{1,0:T(8,128)(2,1)}), bf16[2048,512]{1,0:T(8,128)(2,1)}) %all-gather.17.cloned.1.call-update) | async-done | bytes 2097168 | tf_op jit(solution)/shard_map/all_gather | solution.py:89
  152.6 33.5 %all-gather.13.cloned.1.call-done = bf16[2048,512]{1,0:T(8,128)(2,1)} async-done(((bf16[256,512]{1,0:T(8,128)(2,1)}), bf16[2048,512]{1,0:T(8,128)(2,1)}) %all-gather.13.cloned.1.call-update) | async-done | bytes 2097168 | tf_op jit(solution)/shard_map/all_gather | solution.py:90
  191.0 44.9 %all-gather.19.cloned.1.call-done = bf16[2048,512]{1,0:T(8,128)(2,1)} async-done(((bf16[256,512]{1,0:T(8,128)(2,1)}), bf16[2048,512]{1,0:T(8,128)(2,1)}) %all-gather.19.cloned.1.call-update) | async-done | bytes 2097168 | tf_op jit(solution)/shard_map/all_gather | solution.py:138
  254.3 44.8 %collective-permute-done = bf16[256,16,256]{2,0,1:T(8,128)(2,1)S(1)} collective-permute-done((bf16[256,16,256]{2,0,1:T(8,128)(2,1)S(1)}, bf16[256,16,256]{2,0,1:T(8,128)(2,1)S(1)}, u32[]{:S(2)}, u32[]{:S(2)}) %collective-permute-start) | collective-permute-done | bytes 2097184 | tf_op jit(solution)/shard_map/ppermute | solution.py:173
  302.3 149.0 %collective-permute-done.1 = bf16[512,16,256]{2,0,1:T(8,128)(2,1)S(1)} collective-permute-done((bf16[512,16,256]{2,0,1:T(8,128)(2,1)S(1)}, bf16[512,16,256]{2,0,1:T(8,128)(2,1)S(1)}, u32[]{:S(2)}, u32[]{:S(2)}) %collective-permute-start.1) | collective-permute-done | bytes 4194336 | tf_op jit(solution)/shard_map/ppermute | solution.py:173
  495.6 34.4 %gather_fusion.2 = f32[4352,2048]{1,0:T(8,128)} fusion(f32[513,2048]{1,0:T(8,128)} %concatenate.51, s32[5120]{0:T(1024)S(1)} %pad_clamp_fusion), kind=kCustom, calls=%fused_computation.2 | custom fusion | bytes 71320576 | tf_op jit(solution)/shard_map/gather | solution.py:156
  536.2 33.0 %gather_fusion.4 = f32[4096]{0:T(1024)S(1)} fusion(f32[512,16]{0,1:T(8,128)S(1)} %fusion.52, s32[4096]{0:T(1024)S(1)} %reshape.331), kind=kCustom, calls=%fused_computation.4 | custom fusion | bytes 65536 | tf_op jit(solution)/shard_map/jvp(jit(take_along_axis))/gather | solution.py:145
  569.8 22.8 gather_fusion
  595.1 17.3 gather_fusion.1
  617.5 495.6 %collective-permute-done.2 = bf16[1024,16,256]{2,0,1:T(8,128)(2,1)} collective-permute-done((bf16[1024,16,256]{2,0,1:T(8,128)(2,1)}, bf16[1024,16,256]{2,0,1:T(8,128)(2,1)}, u32[]{:S(2)}, u32[]{:S(2)}) %collective-permute-start.2) | collective-permute-done | bytes 8388640 | tf_op jit(solution)/shard_map/ppermute | solution.py:173
  1172.6 22.4 multiply_convert_fusion.3
  1195.1 18.9 fusion.75
  1213.9 31.1 %convolution_add_fusion = f32[16,272,2048]{2,1,0:T(8,128)} fusion(f32[16,272,2048]{2,1,0:T(8,128)} %fusion.75, bf16[16,272,256]{2,1,0:T(8,128)(2,1)} %get-tuple-element.104, bf16[2048,16,256]{2,0,1:T(8,128)(2,1)} %all-gather.23.cloned.1.call-done), kind=kOutput, calls=%fused_computation.12 | convolution fusion | flops 4572315648 | bytes 90308608 | tf_op jit(solution)/shard_map/ecf,def->ecd/dot_general | solution.py:202
  1245.1 60.8 %scatter_custom_fusion.2 = f32[513,2048]{1,0:T(8,128)} fusion(s32[4352]{0:T(1024)} %copy-done.56, f32[4352,2048]{1,0:T(8,128)} %bitcast.147, f32[]{:T(128)} %constant.57.clone.1), kind=kCustom, calls=%fused_computation.61 | custom fusion | flops 8912896 | bytes 4203008 | tf_op jit(solution)/shard_map/scatter-add | solution.py:206
  1309.7 30.9 %multiply_reduce_fusion = (bf16[16,272]{1,0:T(8,128)(2,1)S(1)}, f32[16,272,2048]{2,1,0:T(8,128)}) fusion(f32[16,272,2048]{2,1,0:T(8,128)} %bitcast.141, bf16[16,272,256]{2,1,0:T(8,128)(2,1)S(1)} %get-tuple-element.106, bf16[4096,16,256]{2,0,1:T(8,128)(2,1)} %constant_dynamic-update-slice_fusion, s32[]{:T(128)S(6)} %select_n.72), kind=kOutput, calls=%fused_computation.10 | convolution fusion | flops 4581224448 | bytes 90317312 | tf_op jit(solution)/shard_map/ecf,def->ecd/dot_general | solution.py:179
  1340.6 26.8 bitcast_multiply_fusion
  1367.6 25.6 gather_fusion.3
  1406.3 22.1 scatter_custom_fusion.3
  1428.5 60.9 %scatter_custom_fusion.1 = f32[513,2048]{1,0:T(8,128)} fusion(s32[4352]{0:T(1024)} %copy-done.56, f32[4352,2048]{1,0:T(8,128)} %bitcast_multiply_fusion, f32[]{:T(128)} %constant.57.clone.1), kind=kCustom, calls=%fused_computation.63 | custom fusion | flops 8912896 | bytes 4203008 | tf_op jit(solution)/shard_map/scatter-add | solution.py:185
  1542.0 20.5 convert_bitcast_fusion
  1562.6 18.8 convert_bitcast_fusion.2
  1581.8 19.0 convert_bitcast_fusion.1
  1604.9 50.9 %all-reduce.21.cloned.1.call-done = (bf16[512,2048]{1,0:T(8,128)(2,1)}, bf16[512,2048]{1,0:T(8,128)(2,1)}) async-done(((bf16[512,2048]{1,0:T(8,128)(2,1)}, bf16[512,2048]{1,0:T(8,128)(2,1)}), (bf16[512,2048]{1,0:T(8,128)(2,1)}, bf16[512,2048]{1,0:T(8,128)(2,1)})) %all-reduce.21.cloned.1.call-update) | async-done | bytes 4194320 | tf_op jit(solution)/shard_map/psum | solution.py:211
  1661.1 21.7 all-reduce.8
  1690.6 37.3 %reduce-scatter.12.cloned.1.call-done = bf16[256,512]{1,0:T(8,128)(2,1)} async-done(((bf16[2048,512]{1,0:T(8,128)(2,1)}), bf16[256,512]{1,0:T(8,128)(2,1)}) %reduce-scatter.12.cloned.1.call-update) | async-done | bytes 262160 | tf_op jit(solution)/shard_map/reduce_scatter | solution.py:324
  1729.7 68.6 %reduce-scatter.10.cloned.1.call-done = bf16[256,512]{1,0:T(8,128)(2,1)} async-done(((bf16[2048,512]{1,0:T(8,128)(2,1)}), bf16[256,512]{1,0:T(8,128)(2,1)}) %reduce-scatter.10.cloned.1.call-update) | async-done | bytes 262160 | tf_op jit(solution)/shard_map/reduce_scatter | solution.py:321
  1800.1 68.8 %reduce-scatter.8.cloned.1.call-done = bf16[256,512]{1,0:T(8,128)(2,1)} async-done(((bf16[2048,512]{1,0:T(8,128)(2,1)}), bf16[256,512]{1,0:T(8,128)(2,1)}) %reduce-scatter.8.cloned.1.call-update) | async-done | bytes 262160 | tf_op jit(solution)/shard_map/reduce_scatter | solution.py:318
  1870.6 68.7 %reduce-scatter.14.cloned.1.call-done = bf16[256,512]{1,0:T(8,128)(2,1)} async-done(((bf16[2048,512]{1,0:T(8,128)(2,1)}), bf16[256,512]{1,0:T(8,128)(2,1)}) %reduce-scatter.14.cloned.1.call-update) | async-done | bytes 262160 | tf_op jit(solution)/shard_map/reduce_scatter | solution.py:327
  1941.2 284.1 %reduce-scatter.20.cloned.1.call-done = bf16[256,16,256]{0,2,1:T(8,128)(2,1)} async-done(((bf16[2048,16,256]{0,2,1:T(8,128)(2,1)}), bf16[256,16,256]{0,2,1:T(8,128)(2,1)}) %reduce-scatter.20.cloned.1.call-update) | async-done | bytes 2097168 | tf_op jit(solution)/shard_map/reduce_scatter | solution.py:336
  2230.1 280.8 %reduce-scatter.16.cloned.1.call-done = bf16[256,16,256]{0,2,1:T(8,128)(2,1)} async-done(((bf16[2048,16,256]{0,2,1:T(8,128)(2,1)}), bf16[256,16,256]{0,2,1:T(8,128)(2,1)}) %reduce-scatter.16.cloned.1.call-update) | async-done | bytes 2097168 | tf_op jit(solution)/shard_map/reduce_scatter | solution.py:330
  2515.6 281.4 %reduce-scatter.18.cloned.1.call-done = bf16[256,16,256]{0,2,1:T(8,128)(2,1)} async-done(((bf16[2048,16,256]{0,2,1:T(8,128)(2,1)}), bf16[256,16,256]{0,2,1:T(8,128)(2,1)}) %reduce-scatter.18.cloned.1.call-update) | async-done | bytes 2097168 | tf_op jit(solution)/shard_map/reduce_scatter | solution.py:333
  (364 shorter events, 302.1 us)
Async XLA Ops:
  7.2 526.7 %copy-start = (bf16[2048,16]{0,1:T(8,128)(2,1)S(1)}, bf16[2048,16]{0,1:T(8,128)(2,1)}, u32[]{:S(2)}) copy-start(bf16[2048,16]{0,1:T(8,128)(2,1)} %param.28) | copy-start | bytes 196612
  7.2 27.7 all-gather.11.cloned.1.call-start
  7.9 78.4 %all-gather.15.cloned.1.call-start = ((), (), s32[]{:S(2)}) async-start(), calls=%async_computation.9 | async-start | bytes 2359296 | tf_op jit(solution)/shard_map/all_gather | solution.py:88
  8.7 127.6 %all-gather.17.cloned.1.call-start = ((), (), s32[]{:S(2)}) async-start(), calls=%async_computation.10 | async-start | bytes 2359296 | tf_op jit(solution)/shard_map/all_gather | solution.py:89
  9.4 176.7 %all-gather.13.cloned.1.call-start = ((), (), s32[]{:S(2)}) async-start(), calls=%async_computation.8 | async-start | bytes 2359296 | tf_op jit(solution)/shard_map/all_gather | solution.py:90
  10.0 225.9 %all-gather.19.cloned.1.call-start = ((), (), s32[]{:S(2)}) async-start(), calls=%async_computation.11 | async-start | bytes 2359296 | tf_op jit(solution)/shard_map/all_gather | solution.py:138
  10.6 480.9 %all-gather.25.cloned.1.call-start = ((), (), s32[]{:S(2)}) async-start(), calls=%async_computation.15 | async-start | bytes 2621440 | tf_op jit(solution)/shard_map/all_gather | solution.py:74
  11.2 519.4 %all-reduce.15.cloned.1.call-start = ((), (), s32[]{:S(2)}) async-start(), calls=%async_computation.12 | async-start | bytes 8388608 | tf_op jit(solution)/shard_map/psum | solution.py:140
  18.0 168.1 %copy-start.69 = (f32[4,1,512]{2,1,0:T(1,128)}, f32[4,1,512]{2,1,0:T(1,128)S(1)}, u32[]{:S(2)}) copy-start(f32[4,1,512]{2,1,0:T(1,128)S(1)} %convert_element_type.261) | copy-start | bytes 24580
  18.7 127.8 %copy-start.61 = (f32[512]{0:T(512)}, f32[512]{0:T(512)S(1)}, u32[]{:S(2)}) copy-start(f32[512]{0:T(512)S(1)} %convert_element_type.200) | copy-start | bytes 6148
  19.4 127.4 %copy-start.63 = (f32[512]{0:T(512)}, f32[512]{0:T(512)S(1)}, u32[]{:S(2)}) copy-start(f32[512]{0:T(512)S(1)} %convert_element_type.202) | copy-start | bytes 6148
  37.0 149.1 %copy-start.75 = (f32[512]{0:T(512)}, f32[512]{0:T(512)S(1)}, u32[]{:S(2)}) copy-start(f32[512]{0:T(512)S(1)} %fusion.61) | copy-start | bytes 6148
  240.8 893.0 %all-gather.21.cloned.1.call-start = ((), (), s32[]{:S(2)}) async-start(), calls=%async_computation.13 | async-start | bytes 18874368 | tf_op jit(solution)/shard_map/all_gather | solution.py:158
  244.6 912.8 %all-gather.23.cloned.1.call-start = ((), (), s32[]{:S(2)}) async-start(), calls=%async_computation.14 | async-start | bytes 18874368 | tf_op jit(solution)/shard_map/all_gather | solution.py:159
  248.7 1246.2 %all-reduce.17.cloned.1.call-start = ((), (), s32[]{:S(2)}) async-start(), calls=%async_computation.16 | async-start | bytes 4194304 | tf_op jit(solution)/shard_map/psum | solution.py:210
  252.6 46.6 %collective-permute-start = (bf16[256,16,256]{2,0,1:T(8,128)(2,1)S(1)}, bf16[256,16,256]{2,0,1:T(8,128)(2,1)S(1)}, u32[]{:S(2)}, u32[]{:S(2)}) collective-permute-start(bf16[256,16,256]{2,0,1:T(8,128)(2,1)S(1)} %get-tuple-element.108), channel_id=1, source_target_pairs={{0,28},{4,0},{8,4},{12,8},{16,12},{20,16},{24,20},{28,24},{1,29},{... | collective-permute-start | bytes 6291464 | tf_op jit(solution)/shard_map/ppermute | solution.py:173
  299.2 156.5 %copy-start.13 = (bf16[256,16,256]{2,0,1:T(8,128)(2,1)}, bf16[256,16,256]{2,0,1:T(8,128)(2,1)S(1)}, u32[]{:S(2)}) copy-start(bf16[256,16,256]{2,0,1:T(8,128)(2,1)S(1)} %collective-permute-done) | copy-start | bytes 6291460
  299.5 158.5 %copy-start.46 = (s32[512,8]{0,1:T(8,128)S(1)}, s32[512,8]{0,1:T(8,128)}, u32[]{:S(2)}) copy-start(s32[512,8]{0,1:T(8,128)} %param.19) | copy-start | bytes 49156
  299.6 158.9 %copy-start.82 = (bf16[512]{0:T(512)(128)(2,1)S(1)}, bf16[512]{0:T(512)(128)(2,1)}, u32[]{:S(2)}) copy-start(bf16[512]{0:T(512)(128)(2,1)} %param.27) | copy-start | bytes 3076
  299.6 151.8 %collective-permute-start.1 = (bf16[512,16,256]{2,0,1:T(8,128)(2,1)S(1)}, bf16[512,16,256]{2,0,1:T(8,128)(2,1)S(1)}, u32[]{:S(2)}, u32[]{:S(2)}) collective-permute-start(bf16[512,16,256]{2,0,1:T(8,128)(2,1)S(1)} %pad_maximum_fusion.1), channel_id=1, source_target_pairs={{0,24},{4,28},{8,0},{12,4},{16,8},{20,12},{24,16},{28,20},{1,25},{... | collective-permute-start | bytes 12582920 | tf_op jit(solution)/shard_map/ppermute | solution.py:173
  455.9 657.2 %collective-permute-start.2 = (bf16[1024,16,256]{2,0,1:T(8,128)(2,1)}, bf16[1024,16,256]{2,0,1:T(8,128)(2,1)}, u32[]{:S(2)}, u32[]{:S(2)}) collective-permute-start(bf16[1024,16,256]{2,0,1:T(8,128)(2,1)} %pad_maximum_fusion), channel_id=1, source_target_pairs={{0,16},{4,20},{8,24},{12,28},{16,0},{20,4},{24,8},{28,12},{1,17},{... | collective-permute-start | bytes 25165832 | tf_op jit(solution)/shard_map/ppermute | solution.py:173
  593.3 579.3 %copy-start.53 = (f32[16,272]{1,0:T(8,128)}, f32[16,272]{1,0:T(8,128)S(1)}, u32[]{:S(2)}) copy-start(f32[16,272]{1,0:T(8,128)S(1)} %mul.490) | copy-start | bytes 52228
  617.5 503.3 %copy-start.20 = (bf16[256,16,256]{2,1,0:T(8,128)(2,1)S(1)}, bf16[256,16,256]{2,1,0:T(8,128)(2,1)}, u32[]{:S(2)}) copy-start(bf16[256,16,256]{2,1,0:T(8,128)(2,1)} %param.31) | copy-start | bytes 6291460
  1309.7 293.7 %all-reduce.19.cloned.1.call-start = ((), (), s32[]{:S(2)}) async-start(), calls=%async_computation.21 | async-start | bytes 131072 | tf_op jit(solution)/shard_map/psum | solution.py:297
  1494.4 161.4 %all-reduce.21.cloned.1.call-start = ((), (), s32[]{:S(2)}) async-start(), calls=%async_computation.25 | async-start | bytes 8388608 | tf_op jit(solution)/shard_map/psum | solution.py:211
  1526.4 201.4 %reduce-scatter.12.cloned.1.call-start = ((), (), s32[]{:S(2)}) async-start(), calls=%async_computation.19 | async-start | bytes 2359296 | tf_op jit(solution)/shard_map/reduce_scatter | solution.py:324
  1530.9 267.4 %reduce-scatter.10.cloned.1.call-start = ((), (), s32[]{:S(2)}) async-start(), calls=%async_computation.18 | async-start | bytes 2359296 | tf_op jit(solution)/shard_map/reduce_scatter | solution.py:321
  1533.8 335.0 %reduce-scatter.8.cloned.1.call-start = ((), (), s32[]{:S(2)}) async-start(), calls=%async_computation.17 | async-start | bytes 2359296 | tf_op jit(solution)/shard_map/reduce_scatter | solution.py:318
  1536.8 402.6 %reduce-scatter.14.cloned.1.call-start = ((), (), s32[]{:S(2)}) async-start(), calls=%async_computation.20 | async-start | bytes 2359296 | tf_op jit(solution)/shard_map/reduce_scatter | solution.py:327
  1541.7 683.6 %reduce-scatter.20.cloned.1.call-start = ((), (), s32[]{:S(2)}) async-start(), calls=%async_computation.24 | async-start | bytes 18874368 | tf_op jit(solution)/shard_map/reduce_scatter | solution.py:336
  1562.5 948.3 %reduce-scatter.16.cloned.1.call-start = ((), (), s32[]{:S(2)}) async-start(), calls=%async_computation.22 | async-start | bytes 18874368 | tf_op jit(solution)/shard_map/reduce_scatter | solution.py:330
  1581.5 1215.6 %reduce-scatter.18.cloned.1.call-start = ((), (), s32[]{:S(2)}) async-start(), calls=%async_computation.23 | async-start | bytes 18874368 | tf_op jit(solution)/shard_map/reduce_scatter | solution.py:333
  (75 other events, 1125.0 us)
Sparse Core Ops, SparseCore 0:
  9.6 25.2 all-gather.10
  37.0 49.2 all-gather.14
  88.5 47.7 all-gather.16
  138.3 47.7 all-gather.12
  188.1 47.7 all-gather.18
  237.3 21.0 all-gather.24
  261.3 85.4 all-reduce.14
  349.3 513.8 all-gather.20
  865.6 291.8 all-gather.22
  1309.8 57.4 all-reduce.16
  1494.5 73.3 all-reduce.18
  1570.1 85.6 all-reduce.20
  1659.7 68.0 reduce-scatter.11
  1731.6 66.5 reduce-scatter.9
  1802.1 66.7 reduce-scatter.7
  1872.6 66.7 reduce-scatter.13
  1943.5 281.7 reduce-scatter.19
  2229.0 281.8 reduce-scatter.15
  2515.1 281.8 reduce-scatter.17
